TPU v7x, 512 devices: a whole 4x8x8 slice. The times are simulated.
512 devices in a mesh: dom: 128 (over y, z, core), scen: 4 (over x).
Axes of the slice: x: 4, y: 8, z: 8, core: 2. Of those that a mesh axis runs over, the one named last changes fastest.
Arguments:
- embedding: bfloat16 [1310720, 256], P(('dom', 'scen')), may hold values from -6 to 6
- scenario_feats: bfloat16 [16, 1310720], P(None, ('dom', 'scen')), may hold values from -6 to 6
- adjacency: bfloat16 [10240, 2, 128, 128], P(('dom', 'scen')), may hold values from -0.3125 to 0.3125
- driver_weight: bfloat16 [1310720, 128], P(('dom', 'scen')), may hold values from -0.3125 to 0.3125
- local_slot: int32 [10240], P(('dom', 'scen')), may hold values from 0 to 79, as said below
- halo_slot: int32 [10240], P(('dom', 'scen')), may hold values from 0 to 15, as said below
- send_rows: int32 [65536, 16], P(('dom', 'scen')), may hold values from 0 to 2559
- send_count: int32 [65536], P(('dom', 'scen')), may hold values from 1 to 16, as said below
- hot_ids: int32 [128], replicated, may hold values from 0 to 1310719, as said below
- first_weight: bfloat16 [512, 256], P('scen'), may hold values from -0.25 to 0.25
- feature_weight: bfloat16 [16, 256], replicated, may hold values from -1.5 to 1.5
- first_bias: float32 [256], replicated, may hold values from -3 to 3
- second_weight: bfloat16 [256, 256], P('scen'), may hold values from -0.375 to 0.375
- second_bias: float32 [256], replicated, may hold values from -3 to 3
Outputs:
- updated: bfloat16 [1310720, 256], P(('dom', 'scen'))
Inputs may be any that keep to these rules, and one draw needn't show every extreme that they name: `local_slot`: the 20 entries of one device are distinct and name exactly 5 tiles of each device of its partition; values s * 20 to s * 20 + 19 are tiles of scen index s. `halo_slot`: the entries of one device name every halo tile at least once. `send_count`: every device has a partition to which it sends 16 pins. `hot_ids`: no device holds more than 1 of them, and some device holds exactly that many.
All inputs are finite; a program needn't handle non-finite values.
Results may differ from a plain program's by a relative error of at most 0.0038.
Values may be sent and summed in bfloat16 or wider, within the bound.
No kernel may reach another device: no remote copies, remote signals or barrier semaphores. Data moves between devices by JAX's collectives and lax.ppermute only.
A program may use at most 64 MiB of HBM per device.

v0:
```python
import jax
import jax.numpy as jnp
from jax import lax
from jax.sharding import PartitionSpec as P


def per_device(
    embedding,
    scenario_feats,
    adjacency,
    driver_weight,
    local_slot,
    halo_slot,
    send_rows,
    send_count,
    hot_ids,
    first_weight,
    feature_weight,
    first_bias,
    second_weight,
    second_bias,
):
    rows, width = embedding.shape
    tile = adjacency.shape[-1]
    tiles = rows // tile
    groups = lax.axis_size("scen")
    partition = lax.all_gather(embedding, "scen", axis=0, tiled=True)
    local_tiles = partition.reshape(groups * tiles, tile, width)[local_slot]
    slots_per_peer = send_rows.shape[1]
    live = jnp.arange(slots_per_peer, dtype=jnp.int32)[None, :] < send_count[:, None]
    outgoing_rows = jnp.where(
        live[:, :, None], embedding[send_rows], jnp.zeros((), embedding.dtype)
    )
    incoming = lax.all_to_all(outgoing_rows, "dom", split_axis=0, concat_axis=0, tiled=True)
    halo_tiles = incoming.reshape(-1, tile, width)[halo_slot]
    myself = lax.axis_index(("dom", "scen"))
    owner = hot_ids // rows
    within = hot_ids - owner * rows
    mine = jnp.where(
        (owner == myself)[:, None], embedding[within].astype(jnp.float32), jnp.float32(0.0)
    )
    drivers = lax.psum(mine, ("dom", "scen")).astype(jnp.bfloat16)
    summed = jnp.einsum(
        "tij,tjc->tic", adjacency[:, 0], local_tiles, preferred_element_type=jnp.float32
    )
    summed = summed + jnp.einsum(
        "tij,tjc->tic", adjacency[:, 1], halo_tiles, preferred_element_type=jnp.float32
    )
    summed = summed.reshape(rows, width) + jnp.dot(
        driver_weight, drivers, preferred_element_type=jnp.float32
    )
    aggregate = summed.astype(jnp.bfloat16)
    joined = jnp.concatenate([embedding, aggregate], axis=1)
    starting = (
        jnp.dot(scenario_feats.T, feature_weight, preferred_element_type=jnp.float32) + first_bias
    )
    columns = joined
    inner = starting + jnp.dot(
        columns,
        lax.all_gather(first_weight, "scen", axis=0, tiled=True),
        preferred_element_type=jnp.float32,
    )
    activated = jax.nn.gelu(inner, approximate=False).astype(jnp.bfloat16)
    residual = embedding.astype(jnp.float32) + second_bias
    columns = activated
    result = residual + jnp.dot(
        columns,
        lax.all_gather(second_weight, "scen", axis=0, tiled=True),
        preferred_element_type=jnp.float32,
    )
    return result.astype(jnp.bfloat16)


def solution(mesh):
    return jax.shard_map(
        per_device,
        mesh=mesh,
        in_specs=(
            P(("dom", "scen"), None),
            P(None, ("dom", "scen")),
            P(("dom", "scen"), None, None, None),
            P(("dom", "scen"), None),
            P(("dom", "scen")),
            P(("dom", "scen")),
            P(("dom", "scen"), None),
            P(("dom", "scen")),
            P(),
            P("scen", None),
            P(),
            P(),
            P("scen", None),
            P(),
        ),
        out_specs=P(("dom", "scen"), None),
        check_vma=False,
    )
```

profile of v0, /device:TPU:8, one launch (start us, length us, event | category | flops | bytes accessed | tf_op | source)
XLA Modules:
  0.0 204.4 jit_solution(11013594092646320890)
XLA Ops:
  6.5 0.7 all-gather.2.cloned.1.call-update
  7.3 0.7 compare_select_fusion
  8.0 0.1 copy.18
  8.1 0.1 reshape.46
  8.2 0.0 copy-start.6
  8.2 7.5 %gather_fusion.1 = bf16[2048,256]{1,0:T(8,128)(2,1)S(1)} fusion(bf16[2560,256]{1,0:T(8,128)(2,1)S(1)} %copy-done.1, s32[2048]{0:T(1024)S(1)} %broadcast_clamp_fusion), kind=kCustom, calls=%fused_computation.1 | custom fusion | bytes 2105344 | tf_op jit(solution)/shard_map/gather | solution.py:32
  15.7 0.0 copy-start.7
  15.7 0.1 iota_compare_fusion
  15.8 0.0 copy-start.5
  15.8 0.0 copy-start.4
  15.8 1.2 broadcast_select_fusion
  17.1 17.4 %all-to-all-start = ((bf16[128,16,256]{2,1,0:T(8,128)(2,1)}), bf16[128,16,256]{2,1,0:T(8,128)(2,1)S(1)}, u32[]{:S(2)}, u32[]{:S(2)}) async-start(bf16[128,16,256]{2,1,0:T(8,128)(2,1)} %broadcast_select_fusion), calls=%async_computation | async-start | bytes 2097152 | tf_op jit(solution)/shard_map/all_to_all | solution.py:34
  34.5 0.8 gather_fusion.3
  35.3 0.1 convert_select_fusion
  35.4 114.3 %all-reduce.1 = bf16[128,256]{1,0:T(8,128)(2,1)S(1)} all-reduce(f32[128,256]{1,0:T(8,128)S(1)} %convert_select_fusion), channel_id=1, replica_groups=mesh['dom'=128,'scen'=4] {'dom','scen'}, use_global_device_ids=true, to_apply=%region_0.1 | all-reduce | flops 32768 | bytes 196608 | tf_op jit(solution)/shard_map/psum | solution.py:42
  149.8 12.2 %all_gather.11 = bf16[256,256]{1,0:T(8,128)(2,1)S(1)} all-gather(bf16[64,256]{1,0:T(8,128)(2,1)} %param.26), channel_id=1, replica_groups=mesh['dom'=128,'scen'=4] {'scen'}, dimensions={0}, use_global_device_ids=true | all-gather | bytes 163840 | tf_op jit(solution)/shard_map/all_gather | solution.py:68
  162.0 13.2 %all_gather.10 = bf16[512,256]{1,0:T(8,128)(2,1)} all-gather(bf16[128,256]{1,0:T(8,128)(2,1)S(1)} %copy-done.5), channel_id=1, replica_groups=mesh['dom'=128,'scen'=4] {'scen'}, dimensions={0}, use_global_device_ids=true | all-gather | bytes 327680 | tf_op jit(solution)/shard_map/all_gather | solution.py:60
  175.1 0.7 compare_select_fusion.2
  175.8 0.7 compare_select_fusion.3
  176.4 0.6 pad_clamp_fusion.2
  177.0 2.7 %convolution_add_fusion.2 = f32[2560,256]{1,0:T(8,128)} fusion(bf16[16,2560]{1,0:T(8,128)(2,1)S(1)} %copy-done.4, bf16[16,256]{1,0:T(8,128)(2,1)} %param.24, f32[256]{0:T(256)} %param.25), kind=kOutput, calls=%fused_computation.6 | convolution fusion | flops 21626880 | bytes 2712576 | tf_op jit(solution)/shard_map/dot_general | solution.py:55
  179.8 1.8 gather_fusion.2
  181.5 3.2 %gather_fusion = bf16[20,128,256]{2,1,0:T(8,128)(2,1)S(1)} fusion(bf16[80,128,256]{2,1,0:T(8,128)(2,1)} %bitcast.33, s32[1024]{0:T(1024)} %pad_clamp_fusion.2), kind=kCustom, calls=%fused_computation | custom fusion | bytes 2621520 | tf_op jit(solution)/shard_map/gather | solution.py:28
  184.8 0.0 copy-start.2
  184.8 0.0 copy-start.3
  184.8 1.7 fusion.52
  186.6 0.1 copy-done.3
  186.7 0.5 convolution_add_fusion.3
  187.2 0.0 copy-start.8
  187.2 0.5 fusion.1
  187.7 0.2 copy-done.8
  187.9 9.7 %fusion.2 = bf16[2560,256]{1,0:T(8,128)(2,1)} fusion(bf16[256,256]{1,0:T(8,128)(2,1)S(1)} %all_gather.11, bf16[2560,256]{1,0:T(8,128)(2,1)S(1)} %copy-done.1, f32[256]{0:T(256)S(1)} %copy-done.8, f32[2560,256]{1,0:T(8,128)} %convolution_add_fusion.2, bf16[512,256]{1,0:T(8,128)(2,1)} %all_gather.10, bf16[2560,256]{1,0:T(8,128)(2,1)S(1)} %fusion.1), kind=kOutput, calls=%fused_computation.11 | convolution fusion | flops 1057751040 | bytes 6947840 | tf_op jit(solution)/shard_map/dot_general | solution.py:66
  (17 shorter events, 0.1 us)
Async XLA Ops:
  6.5 180.7 %copy-start = (bf16[2560,128]{1,0:T(8,128)(2,1)S(1)}, bf16[2560,128]{1,0:T(8,128)(2,1)}, u32[]{:S(2)}) copy-start(bf16[2560,128]{1,0:T(8,128)(2,1)} %param.17) | copy-start | bytes 1966084
  6.5 1.6 copy-start.1
  6.5 175.0 %all-gather.2.cloned.1.call-start = ((), (), s32[]{:S(2)}) async-start(), calls=%async_computation.1 | async-start | bytes 6553600 | tf_op jit(solution)/shard_map/all_gather | solution.py:27
  8.2 7.5 %copy-start.6 = (s32[128]{0:T(128)S(1)}, s32[128]{0:T(128)}, u32[]{:S(2)}) copy-start(s32[128]{0:T(128)} %param.21) | copy-start | bytes 1540
  15.7 18.8 %copy-start.7 = (s32[128]{0:T(128)S(1)}, s32[128]{0:T(128)}, u32[]{:S(2)}) copy-start(s32[128]{0:T(128)} %param.22) | copy-start | bytes 1540
  15.8 146.2 %copy-start.5 = (bf16[128,256]{1,0:T(8,128)(2,1)S(1)}, bf16[128,256]{1,0:T(8,128)(2,1)}, u32[]{:S(2)}) copy-start(bf16[128,256]{1,0:T(8,128)(2,1)} %param.23) | copy-start | bytes 196612
  15.8 161.2 %copy-start.4 = (bf16[16,2560]{1,0:T(8,128)(2,1)S(1)}, bf16[16,2560]{1,0:T(8,128)(2,1)}, u32[]{:S(2)}) copy-start(bf16[16,2560]{1,0:T(8,128)(2,1)} %param.15) | copy-start | bytes 245764
  17.1 162.7 %all-to-all-start = ((bf16[128,16,256]{2,1,0:T(8,128)(2,1)}), bf16[128,16,256]{2,1,0:T(8,128)(2,1)S(1)}, u32[]{:S(2)}, u32[]{:S(2)}) async-start(bf16[128,16,256]{2,1,0:T(8,128)(2,1)} %broadcast_select_fusion), calls=%async_computation | async-start | bytes 2097152 | tf_op jit(solution)/shard_map/all_to_all | solution.py:34
  184.8 1.8 copy-start.2
  184.8 1.9 copy-start.3
  187.2 0.7 copy-start.8
Sparse Core Ops, SparseCore 0:
  9.5 66.8 all-gather.1
where the time goes:
time: 205 us; the launch traced here: 204 us
  blocking collectives  140 us (68%)
  starting transfers between devices  17.4 us (8%)
  matrix products  15.1 us (7%)
  local copies, waits for them, and re-layouts  13.9 us (7%)
  between operations  13.6 us (7%)
  other arithmetic  4.05 us (2%)
    psum x1, blocking collectives, per_device(): drivers = lax.psum(mine, ('dom', 'scen')).astype(jnp.bfloat16)  114 us
    all_to_all x1, starting transfers between devices, per_device(): lax.all_to_all(outgoing_rows, 'dom', split_axis=0, concat_axis=0, tiled=T...  17.4 us
    all_gather x1, blocking collectives, per_device(): lax.all_gather(first_weight, 'scen', axis=0, tiled=True)  13.2 us
    all_gather x1, blocking collectives, per_device(): lax.all_gather(second_weight, 'scen', axis=0, tiled=True)  12.2 us
    dot_general x1, matrix products, per_device(): jnp.dot(columns, lax.all_gather(second_weight, 'scen', axis=0, tiled=True...  9.68 us
    gather x1, local copies, waits for them, and re-layouts, per_device(): embedding[send_rows]  7.5 us
  transfers between devices with their start and end apart: 2, of which 0 were waited for; matrix products, arithmetic and copies ran while one was open for 8% of the time, Pallas kernels for 0%

commit v1 on v0

--- a/solution.py
+++ b/solution.py
@@ -2,6 +2,19 @@
 import jax.numpy as jnp
 from jax import lax
 from jax.sharding import PartitionSpec as P
+
+
+def ring_gather(shard, axis, dim):
+    ways = lax.axis_size(axis)
+    up = [(d, (d + 1) % ways) for d in range(ways)]
+    down = [(d, (d - 1) % ways) for d in range(ways)]
+    earlier, later = ([shard], [shard])
+    for _ in range(ways // 2):
+        earlier.append(lax.ppermute(earlier[-1], axis, up))
+    for _ in range((ways - 1) // 2):
+        later.append(lax.ppermute(later[-1], axis, down))
+    line = jnp.concatenate([*earlier[::-1], *later[1:]], axis=dim)
+    return jnp.roll(line, (lax.axis_index(axis) - ways // 2) * shard.shape[dim], axis=dim)
 
 
 def per_device(
@@ -56,9 +69,7 @@
     )
     columns = joined
     inner = starting + jnp.dot(
-        columns,
-        lax.all_gather(first_weight, "scen", axis=0, tiled=True),
-        preferred_element_type=jnp.float32,
+        columns, ring_gather(first_weight, "scen", 0), preferred_element_type=jnp.float32
     )
     activated = jax.nn.gelu(inner, approximate=False).astype(jnp.bfloat16)
     residual = embedding.astype(jnp.float32) + second_bias

time: 205 us -> 199 us (0.971)
  the two profiles are of different devices: /device:TPU:8 before, /device:TPU:24 now
where the time goes in v1:
time: 199 us
  blocking collectives  122 us (61%)
  starting transfers between devices  26.7 us (13%)
  local copies, waits for them, and re-layouts  19 us (10%)
  matrix products  14.4 us (7%)
  between operations  13.7 us (7%)
  other arithmetic  2.16 us (1%)
    psum x1, blocking collectives, per_device(): drivers = lax.psum(mine, ('dom', 'scen')).astype(jnp.bfloat16)  109 us
    all_to_all x1, starting transfers between devices, per_device(): lax.all_to_all(outgoing_rows, 'dom', split_axis=0, concat_axis=0, tiled=T...  17.5 us
    all_gather x1, blocking collectives, per_device(): lax.all_gather(second_weight, 'scen', axis=0, tiled=True)  12.9 us
    dot_general x1, matrix products, per_device(): jnp.dot(columns, lax.all_gather(second_weight, 'scen', axis=0, tiled=True...  9.68 us
    gather x1, local copies, waits for them, and re-layouts, per_device(): embedding[send_rows]  7.5 us
    ppermute x2, starting transfers between devices, ring_gather(): earlier.append(lax.ppermute(earlier[-1], axis, up))  5.59 us
    unnamed x37, local copies, waits for them, and re-layouts  5.02 us
  transfers between devices with their start and end apart: 5, of which 0 were waited for; matrix products, arithmetic and copies ran while one was open for 10% of the time, Pallas kernels for 0%

profile of v1, /device:TPU:24, one launch (start us, length us, event | category | flops | bytes accessed | tf_op | source)
XLA Modules:
  0.0 198.6 jit_solution(8034839225348569814)
XLA Ops:
  6.5 0.7 all-gather.2.cloned.1.call-update
  7.3 3.4 %collective-permute-start = (bf16[128,256]{1,0:T(8,128)(2,1)}, bf16[128,256]{1,0:T(8,128)(2,1)S(1)}, u32[]{:S(2)}, u32[]{:S(2)}) collective-permute-start(bf16[128,256]{1,0:T(8,128)(2,1)} %param.23), channel_id=1, source_target_pairs={{0,1},{1,2},{2,3},{3,0},{4,5},{5,6},{6,7},{7,4},{8,9},{9,10},{10,1... | collective-permute-start | bytes 196616 | tf_op jit(solution)/shard_map/ppermute | solution.py:13
  10.7 3.7 %collective-permute-start.2 = (bf16[128,256]{1,0:T(8,128)(2,1)}, bf16[128,256]{1,0:T(8,128)(2,1)S(1)}, u32[]{:S(2)}, u32[]{:S(2)}) collective-permute-start(bf16[128,256]{1,0:T(8,128)(2,1)} %param.23), channel_id=1, source_target_pairs={{0,3},{1,0},{2,1},{3,2},{4,7},{5,4},{6,5},{7,6},{8,11},{9,8},{10,9... | collective-permute-start | bytes 196616 | tf_op jit(solution)/shard_map/ppermute | solution.py:15
  14.3 0.7 compare_select_fusion
  15.0 0.1 copy.18
  15.1 0.1 reshape.46
  15.2 7.5 %gather_fusion.1 = bf16[2048,256]{1,0:T(8,128)(2,1)S(1)} fusion(bf16[2560,256]{1,0:T(8,128)(2,1)S(1)} %copy-done.1, s32[2048]{0:T(1024)S(1)} %broadcast_clamp_fusion), kind=kCustom, calls=%fused_computation.1 | custom fusion | bytes 2105344 | tf_op jit(solution)/shard_map/gather | solution.py:45
  22.8 0.1 iota_compare_fusion
  22.9 1.2 broadcast_select_fusion
  24.2 17.5 %all-to-all-start = ((bf16[128,16,256]{2,1,0:T(8,128)(2,1)}), bf16[128,16,256]{2,1,0:T(8,128)(2,1)S(1)}, u32[]{:S(2)}, u32[]{:S(2)}) async-start(bf16[128,16,256]{2,1,0:T(8,128)(2,1)} %broadcast_select_fusion), calls=%async_computation | async-start | bytes 2097152 | tf_op jit(solution)/shard_map/all_to_all | solution.py:47
  41.7 0.8 gather_fusion.3
  42.6 0.1 convert_select_fusion
  42.8 2.0 %convolution_add_fusion.2 = f32[2560,256]{1,0:T(8,128)} fusion(bf16[16,2560]{1,0:T(8,128)(2,1)S(1)} %copy-done.6, bf16[16,256]{1,0:T(8,128)(2,1)S(1)} %copy-done.8, f32[256]{0:T(256)S(1)} %copy-done.9), kind=kOutput, calls=%fused_computation.6 | convolution fusion | flops 21626880 | bytes 2712576 | tf_op jit(solution)/shard_map/dot_general | solution.py:68
  44.8 2.2 %collective-permute-start.1 = (bf16[128,256]{1,0:T(8,128)(2,1)S(1)}, bf16[128,256]{1,0:T(8,128)(2,1)S(1)}, u32[]{:S(2)}, u32[]{:S(2)}) collective-permute-start(bf16[128,256]{1,0:T(8,128)(2,1)S(1)} %collective-permute-done), channel_id=1, source_target_pairs={{0,1},{1,2},{2,3},{3,0},{4,5},{5,6},{6,7},{7,4},{8,9},{9,10},{10,1... | collective-permute-start | bytes 196616 | tf_op jit(solution)/shard_map/ppermute | solution.py:13
  47.0 109.0 %all-reduce.1 = bf16[128,256]{1,0:T(8,128)(2,1)S(1)} all-reduce(f32[128,256]{1,0:T(8,128)S(1)} %convert_select_fusion), channel_id=1, replica_groups=mesh['dom'=128,'scen'=4] {'dom','scen'}, use_global_device_ids=true, to_apply=%region_0.1 | all-reduce | flops 32768 | bytes 196608 | tf_op jit(solution)/shard_map/psum | solution.py:55
  156.0 12.9 %all_gather.7 = bf16[256,256]{1,0:T(8,128)(2,1)} all-gather(bf16[64,256]{1,0:T(8,128)(2,1)S(1)} %copy-done.7), channel_id=1, replica_groups=mesh['dom'=128,'scen'=4] {'scen'}, dimensions={0}, use_global_device_ids=true | all-gather | bytes 163840 | tf_op jit(solution)/shard_map/all_gather | solution.py:79
  168.9 0.6 constant_dynamic-update-slice_fusion.7
  169.5 0.6 constant_dynamic-update-slice_fusion.6
  170.1 0.6 constant_dynamic-update-slice_fusion.5
  170.8 0.6 constant_dynamic-update-slice_fusion.4
  171.4 0.6 constant_dynamic-update-slice_fusion.3
  172.0 0.6 constant_dynamic-update-slice_fusion.2
  172.6 0.6 constant_dynamic-update-slice_fusion.1
  173.3 0.6 constant_dynamic-update-slice_fusion
  173.9 1.8 gather_fusion.2
  175.7 3.1 %gather_fusion = bf16[20,128,256]{2,1,0:T(8,128)(2,1)S(1)} fusion(bf16[80,128,256]{2,1,0:T(8,128)(2,1)} %bitcast.32, s32[1024]{0:T(1024)S(1)} %pad_clamp_fusion.2), kind=kCustom, calls=%fused_computation | custom fusion | bytes 2621520 | tf_op jit(solution)/shard_map/gather | solution.py:41
  178.8 1.7 fusion.52
  180.5 0.1 copy-done.3
  180.7 0.5 convolution_add_fusion.3
  181.2 0.5 fusion.1
  181.7 0.4 copy-done.5
  182.1 9.7 %fusion.2 = bf16[2560,256]{1,0:T(8,128)(2,1)} fusion(bf16[256,256]{1,0:T(8,128)(2,1)S(1)} %copy-done.5, bf16[2560,256]{1,0:T(8,128)(2,1)S(1)} %copy-done.1, f32[256]{0:T(256)S(1)} %copy-done.12, f32[2560,256]{1,0:T(8,128)} %convolution_add_fusion.2, bf16[2560,256]{1,0:T(8,128)(2,1)S(1)} %fusion.1, bf16[1024,256]{1,0:T(8,128)(2,1)} %constant_dynamic-update-slice_fusion, ...), kind=kOutput, calls=%fused_computation.11 | convolution fusion | flops 1057751040 | bytes 8258564 | tf_op jit(solution)/shard_map/dot_general | solution.py:77
  (42 shorter events, 0.2 us)
Async XLA Ops:
  6.5 174.7 %copy-start = (bf16[2560,128]{1,0:T(8,128)(2,1)S(1)}, bf16[2560,128]{1,0:T(8,128)(2,1)}, u32[]{:S(2)}) copy-start(bf16[2560,128]{1,0:T(8,128)(2,1)} %param.17) | copy-start | bytes 1966084
  6.5 8.7 %copy-start.1 = (bf16[2560,256]{1,0:T(8,128)(2,1)S(1)}, bf16[2560,256]{1,0:T(8,128)(2,1)}, u32[]{:S(2)}) copy-start(bf16[2560,256]{1,0:T(8,128)(2,1)} %param.14) | copy-start | bytes 3932164
  6.5 169.1 %all-gather.2.cloned.1.call-start = ((), (), s32[]{:S(2)}) async-start(), calls=%async_computation.1 | async-start | bytes 6553600 | tf_op jit(solution)/shard_map/all_gather | solution.py:40
  7.3 37.5 %collective-permute-start = (bf16[128,256]{1,0:T(8,128)(2,1)}, bf16[128,256]{1,0:T(8,128)(2,1)S(1)}, u32[]{:S(2)}, u32[]{:S(2)}) collective-permute-start(bf16[128,256]{1,0:T(8,128)(2,1)} %param.23), channel_id=1, source_target_pairs={{0,1},{1,2},{2,3},{3,0},{4,5},{5,6},{6,7},{7,4},{8,9},{9,10},{10,1... | collective-permute-start | bytes 196616 | tf_op jit(solution)/shard_map/ppermute | solution.py:13
  10.7 160.1 %collective-permute-start.2 = (bf16[128,256]{1,0:T(8,128)(2,1)}, bf16[128,256]{1,0:T(8,128)(2,1)S(1)}, u32[]{:S(2)}, u32[]{:S(2)}) collective-permute-start(bf16[128,256]{1,0:T(8,128)(2,1)} %param.23), channel_id=1, source_target_pairs={{0,3},{1,0},{2,1},{3,2},{4,7},{5,4},{6,5},{7,6},{8,11},{9,8},{10,9... | collective-permute-start | bytes 196616 | tf_op jit(solution)/shard_map/ppermute | solution.py:15
  15.2 7.5 %copy-start.10 = (s32[128]{0:T(128)S(1)}, s32[128]{0:T(128)}, u32[]{:S(2)}) copy-start(s32[128]{0:T(128)} %param.21) | copy-start | bytes 1540
  22.8 18.9 %copy-start.11 = (s32[128]{0:T(128)S(1)}, s32[128]{0:T(128)}, u32[]{:S(2)}) copy-start(s32[128]{0:T(128)} %param.22) | copy-start | bytes 1540
  22.8 19.9 %copy-start.13 = (s32[20]{0:T(128)S(1)}, s32[20]{0:T(128)}, u32[]{:S(2)}) copy-start(s32[20]{0:T(128)} %param.19) | copy-start | bytes 244
  22.8 19.9 %copy-start.14 = (s32[20]{0:T(128)S(1)}, s32[20]{0:T(128)}, u32[]{:S(2)}) copy-start(s32[20]{0:T(128)} %param.18) | copy-start | bytes 244
  22.8 19.9 %copy-start.6 = (bf16[16,2560]{1,0:T(8,128)(2,1)S(1)}, bf16[16,2560]{1,0:T(8,128)(2,1)}, u32[]{:S(2)}) copy-start(bf16[16,2560]{1,0:T(8,128)(2,1)} %param.15) | copy-start | bytes 245764
  22.8 19.9 %copy-start.8 = (bf16[16,256]{1,0:T(8,128)(2,1)S(1)}, bf16[16,256]{1,0:T(8,128)(2,1)}, u32[]{:S(2)}) copy-start(bf16[16,256]{1,0:T(8,128)(2,1)} %param.24) | copy-start | bytes 24580
  22.8 19.9 %copy-start.9 = (f32[256]{0:T(256)S(1)}, f32[256]{0:T(256)}, u32[]{:S(2)}) copy-start(f32[256]{0:T(256)} %param.25) | copy-start | bytes 3076
  24.2 131.8 %copy-start.7 = (bf16[64,256]{1,0:T(8,128)(2,1)S(1)}, bf16[64,256]{1,0:T(8,128)(2,1)}, u32[]{:S(2)}) copy-start(bf16[64,256]{1,0:T(8,128)(2,1)} %param.26) | copy-start | bytes 98308
  24.2 149.7 %all-to-all-start = ((bf16[128,16,256]{2,1,0:T(8,128)(2,1)}), bf16[128,16,256]{2,1,0:T(8,128)(2,1)S(1)}, u32[]{:S(2)}, u32[]{:S(2)}) async-start(bf16[128,16,256]{2,1,0:T(8,128)(2,1)} %broadcast_select_fusion), calls=%async_computation | async-start | bytes 2097152 | tf_op jit(solution)/shard_map/all_to_all | solution.py:47
  41.7 128.5 %copy-start.4 = (bf16[128,256]{1,0:T(8,128)(2,1)S(1)}, bf16[128,256]{1,0:T(8,128)(2,1)}, u32[]{:S(2)}) copy-start(bf16[128,256]{1,0:T(8,128)(2,1)} %param.23) | copy-start | bytes 196612
  44.8 124.1 %collective-permute-start.1 = (bf16[128,256]{1,0:T(8,128)(2,1)S(1)}, bf16[128,256]{1,0:T(8,128)(2,1)S(1)}, u32[]{:S(2)}, u32[]{:S(2)}) collective-permute-start(bf16[128,256]{1,0:T(8,128)(2,1)S(1)} %collective-permute-done), channel_id=1, source_target_pairs={{0,1},{1,2},{2,3},{3,0},{4,5},{5,6},{6,7},{7,4},{8,9},{9,10},{10,1... | collective-permute-start | bytes 196616 | tf_op jit(solution)/shard_map/ppermute | solution.py:13
  178.8 1.8 copy-start.2
  178.8 1.9 copy-start.3
  181.2 0.9 copy-start.5
  181.2 0.9 copy-start.12
Sparse Core Ops, SparseCore 0:
  9.5 68.0 all-gather.1
